TPU v7x, 32 devices: a whole 2x2x4 slice. The times are simulated.
32 devices in a mesh: zone: 4 (over y, x), slab: 8 (over z, core).
Axes of the slice: x: 2, y: 2, z: 4, core: 2. Of those that a mesh axis runs over, the one named last changes fastest.
Arguments:
- tracers: float32 [4, 4, 2048, 2048], P('zone', None, 'slab'), may hold values from -6 to 6
- velocity: float32 [4, 2, 2048, 2048], P('zone', None, 'slab'), may hold values from -0.2 to 0.2
- diffusivity: float32 [4], replicated, may hold values from 0.02 to 0.12
- owner_dev: int32 [512, 2], P('slab'), may hold values from 0 to 23, all different within a row; in each aligned block of 64 rows (0 to 63, 64 to 127, ...) at most 7 rows name the same one
- owner_seg: int32 [512, 2], P('slab'), may hold values from 0 to 63
- intersection: float32 [512, 2], P('slab'), may hold values from 0.2 to 1
Outputs:
- updated: float32 [4, 4, 2048, 2048], P('zone', None, 'slab')
Inputs may be any that keep to these rules, and one draw needn't show every extreme that they name: owner_dev names workpiece slab zone * 8 + slab; the 2 entries of a row differ; the rows of one pin slab name one workpiece slab at most 7 times, and some name one exactly 7 times.
All inputs are finite; a program needn't handle non-finite values.
Results may differ from a plain program's by a relative error of at most 0.00007.
Values sent between devices are 32-bit elements; how exact they have to be, the bound alone decides.
No kernel may reach another device: no remote copies, remote signals or barrier semaphores. Data moves between devices by JAX's collectives and lax.ppermute only.
A program may use at most 128 MiB of HBM per device.

v0:
```python
import jax
import jax.numpy as jnp
from jax import lax
from jax.sharding import PartitionSpec as P

SEG = 32
COUPLE = 0.5


def extended(block, sides, width):
    for axis, dim in sides:
        count = lax.axis_size(axis)
        forward = [(i, i + 1) for i in range(count - 1)]
        backward = [(target, source) for source, target in forward]
        low = lax.ppermute(
            lax.slice_in_dim(block, block.shape[dim] - width, None, axis=dim), axis, forward
        )
        high = lax.ppermute(lax.slice_in_dim(block, 0, width, axis=dim), axis, backward)
        block = jnp.concatenate([low, block, high], axis=dim)
    return block


def from_root(block, axis, owner):
    block = jnp.where(lax.axis_index(axis) == owner, block, jnp.zeros_like(block))
    return lax.psum(block, axis)


def advance(center, upper_row, lower_row, velocity, diffusivity):
    left_cells = jnp.roll(center, 1, axis=3)
    right_cells = jnp.roll(center, -1, axis=3)
    along_rows = velocity[:, 0][:, None]
    along_cols = velocity[:, 1][:, None]
    transport = jnp.maximum(along_rows, 0.0) * (center - upper_row) + jnp.minimum(
        along_rows, 0.0
    ) * (lower_row - center)
    transport = (
        transport
        + jnp.maximum(along_cols, 0.0) * (center - left_cells)
        + jnp.minimum(along_cols, 0.0) * (right_cells - center)
    )
    laplace = upper_row + lower_row + left_cells + right_cells - 4.0 * center
    return center + diffusivity[None, :, None, None] * laplace - transport


def shards(tracers, velocity, diffusivity, owner_dev, owner_seg, intersection):
    zone_count = lax.axis_size("zone")
    slab_count = lax.axis_size("slab")
    zone_index = lax.axis_index("zone")
    padded = extended(tracers, (("slab", 2),), 1)
    stepped = advance(
        padded[:, :, 1:-1], padded[:, :, :-2], padded[:, :, 2:], velocity, diffusivity
    )
    tracer_count = tracers.shape[1]
    row_count = tracers.shape[2]
    col_count = tracers.shape[3]
    seg_count = col_count // SEG
    payload = tracer_count * SEG
    own_face = (
        tracers[0, :, row_count - 1, :]
        .reshape(tracer_count, seg_count, SEG)
        .transpose(1, 0, 2)
        .reshape(seg_count, payload)
    )
    pin_face = from_root(own_face, "zone", zone_count - 1)
    fanout = owner_dev.shape[1]
    item_count = owner_dev.shape[0] * fanout
    target_dev = owner_dev.reshape(item_count)
    target_seg = owner_seg.reshape(item_count)
    weight = intersection.reshape(item_count)
    in_zone = target_dev // slab_count == zone_index
    target_slab = target_dev % slab_count
    pin_values = jnp.repeat(pin_face, fanout, axis=0)
    highest = lax.Precision.HIGHEST
    zone_faces = lax.all_gather(own_face, "slab", axis=0, tiled=True)
    slot_ids = jnp.arange(slab_count * seg_count, dtype=jnp.int32)
    picker = (
        ((target_slab * seg_count + target_seg)[:, None] == slot_ids[None, :]) & in_zone[:, None]
    ).astype(jnp.float32)
    owner_values = jnp.dot(picker, zone_faces, precision=highest)
    item_flux = jnp.where(in_zone, weight, 0.0)[:, None] * (pin_values - owner_values)
    inflow = lax.psum_scatter(
        jnp.dot(picker.T, item_flux, precision=highest), "slab", scatter_dimension=0, tiled=True
    )
    pin_part = jnp.sum(item_flux.reshape(seg_count, fanout, payload), axis=1)
    pin_total = lax.psum(pin_part, "zone")
    is_pin = zone_index == zone_count - 1
    coupling = COUPLE * inflow - jnp.where(is_pin, COUPLE * pin_total, 0.0)
    coupling = (
        coupling.reshape(seg_count, tracer_count, SEG)
        .transpose(1, 0, 2)
        .reshape(tracer_count, col_count)
    )
    return stepped.at[0, :, row_count - 1, :].add(coupling)


def solution(mesh):
    placed = (
        P("zone", None, "slab", None),
        P("zone", None, "slab", None),
        P(),
        P("slab", None),
        P("slab", None),
        P("slab", None),
    )
    return jax.shard_map(
        shards, mesh=mesh, in_specs=placed, out_specs=P("zone", None, "slab", None), check_vma=False
    )
```

profile of v0, /device:TPU:8, one launch (start us, length us, event | category | flops | bytes accessed | tf_op | source)
XLA Modules:
  0.0 117.2 jit_solution(10784930607515676139)
XLA Ops:
  6.5 1.2 slice_reduce_fusion
  7.9 14.4 %all_gather.3 = f32[512,128]{1,0:T(8,128)S(1)} all-gather(f32[64,128]{1,0:T(8,128)S(1)} %copy.61), channel_id=1, replica_groups=mesh['zone'=4,'slab'=8] {'slab'}, dimensions={0}, use_global_device_ids=true | all-gather | bytes 294912 | tf_op jit(solution)/shard_map/all_gather | solution.py:74
  22.4 16.3 %psum.14 = f32[64,128]{1,0:T(8,128)S(1)} all-reduce(f32[64,128]{1,0:T(8,128)S(1)} %broadcast_select_fusion.1), channel_id=1, replica_groups=mesh['zone'=4,'slab'=8] {'zone'}, use_global_device_ids=true, to_apply=%region_1.2 | all-reduce | flops 8192 | bytes 65536 | tf_op jit(solution)/shard_map/psum | solution.py:25
  38.7 0.8 copy.57
  39.5 0.1 reshape.148
  39.6 0.8 copy.59
  40.4 0.1 reshape.150
  40.5 0.8 copy.58
  41.3 0.1 reshape.149
  41.5 0.3 fusion.14
  41.8 1.2 fusion.16
  43.0 1.9 %collective-permute-start = (f32[1,4,1,2048]{3,2,1,0:T(1,128)S(1)}, f32[1,4,1,2048]{3,2,1,0:T(1,128)S(1)}, u32[]{:S(2)}, u32[]{:S(2)}) collective-permute-start(f32[1,4,1,2048]{3,2,1,0:T(1,128)S(1)} %get-tuple-element.21), channel_id=1, source_target_pairs={{0,1},{1,2},{2,3},{3,4},{4,5},{5,6},{6,7},{8,9},{9,10},{10,11},{11... | collective-permute-start | bytes 98312 | tf_op jit(solution)/shard_map/ppermute | solution.py:15
  44.9 3.9 %collective-permute-start.1 = (f32[1,4,1,2048]{3,2,1,0:T(1,128)S(1)}, f32[1,4,1,2048]{3,2,1,0:T(1,128)S(1)}, u32[]{:S(2)}, u32[]{:S(2)}) collective-permute-start(f32[1,4,1,2048]{3,2,1,0:T(1,128)S(1)} %get-tuple-element.20), channel_id=1, source_target_pairs={{1,0},{2,1},{3,2},{4,3},{5,4},{6,5},{7,6},{9,8},{10,9},{11,10},{12... | collective-permute-start | bytes 98312 | tf_op jit(solution)/shard_map/ppermute | solution.py:18
  48.9 13.3 %fusion.28 = (f32[1,4,256,2047]{3,2,1,0:T(8,128)}, f32[1,4,256,2047]{3,2,1,0:T(8,128)}) fusion(f32[1,4,256,2048]{3,2,1,0:T(8,128)} %param.8), kind=kLoop, calls=%fused_computation.47 | loop fusion | bytes 33538048 | tf_op jit(solution)/shard_map/jit(_roll_static)/slice | solution.py:29
  62.1 1.4 %fusion.27 = (f32[1,4,256,1]{3,2,1,0:T(8,128)S(1)}, f32[1,4,256,1]{3,2,1,0:T(8,128)S(1)}) fusion(f32[1,4,256,2048]{3,2,1,0:T(8,128)} %param.8), kind=kLoop, calls=%fused_computation.46 | loop fusion | bytes 16384 | tf_op jit(solution)/shard_map/jit(_roll_static)/slice | solution.py:29
  63.6 2.9 %maximum_bitcast_fusion.1 = (f32[256,2048]{1,0:T(8,128)S(1)}, f32[256,2048]{1,0:T(8,128)}, f32[256,2048]{1,0:T(8,128)}, f32[256,2048]{1,0:T(8,128)}) fusion(f32[1,2,256,2048]{3,2,1,0:T(8,128)S(1)} %copy-done), kind=kLoop, calls=%fused_computation.21 | loop fusion | flops 2097152 | bytes 12582912 | tf_op jit(solution)/shard_map/mul | solution.py:33
  66.5 0.6 fusion.29
  67.1 2.0 %and_reduce_fusion = pred[]{:T(512)} fusion(s32[4]{0:T(128)S(1)} %copy-done.2, s32[1]{0:T(128)} %constant.60.clone.1, s32[1]{0:T(128)} %get-tuple-element.31, s32[1]{0:T(128)} %get-tuple-element.30), kind=kLoop, calls=%fused_computation.36 | loop fusion | flops 27 | bytes 29 | tf_op jit(solution)/shard_map/reduce.1
  69.2 14.3 %psum.15 = f32[64,128]{1,0:T(8,128)S(1)} all-reduce(f32[64,128]{1,0:T(8,128)S(1)} %reduce_sum.9), channel_id=1, replica_groups=mesh['zone'=4,'slab'=8] {'zone'}, use_global_device_ids=true, to_apply=%region_4.5 | all-reduce | flops 8192 | bytes 65536 | tf_op jit(solution)/shard_map/psum | solution.py:85
  83.5 21.2 %fusion.6 = f32[1,4,256,2048]{3,2,1,0:T(8,128)} fusion(f32[1,4,256,2048]{3,2,1,0:T(8,128)} %param.8, f32[1,4,1,2048]{3,2,1,0:T(1,128)S(1)} %collective-permute-done.1, f32[1,4,1,2048]{3,2,1,0:T(1,128)S(1)} %collective-permute-done, f32[1,4,256,1]{3,2,1,0:T(8,128)S(1)} %get-tuple-element.23, f32[1,4,256,2047]{3,2,1,0:T(8,128)} %get-tuple-element.25, ...), kind=kLoop, calls=%fused_computation.7 | loop fusion | flops 48234496 | bytes 42008592 | tf_op jit(solution)/shard_map/sub | solution.py:42
  104.7 0.8 select_subtract_fusion
  105.7 0.1 reshape.156
  105.8 2.2 %broadcast_select_fusion = f32[1,4,1,2048]{3,2,1,0:T(1,128)S(1)} fusion(pred[]{:T(512)} %and_reduce_fusion, f32[1,4,1,2048]{3,2,1,0:T(1,128)S(1)} %reshape.156, f32[1,4,256,2048]{3,2,1,0:T(8,128)} %fusion.6, s32[]{:T(128)} %bitcast.4), kind=kLoop, calls=%fused_computation.31 | loop fusion | flops 16384 | bytes 98309 | tf_op jit(solution)/shard_map/select.1
  108.0 2.4 %scatter-add.4 = f32[1,4,256,2048]{3,2,1,0:T(8,128)} dynamic-update-slice(f32[1,4,256,2048]{3,2,1,0:T(8,128)} %fusion.6, f32[1,4,1,2048]{3,2,1,0:T(1,128)S(1)} %broadcast_select_fusion, s32[]{:T(128)} %constant.58.clone.1, s32[]{:T(128)} %constant.58.clone.1, s32[]{:T(128)} %bitcast.4, s32[]{:T(128)} %constant.58.clone.1) | dynamic-update-slice | bytes 65540 | tf_op jit(solution)/shard_map/scatter-add | solution.py:93
  (22 shorter events, 0.6 us)
Async XLA Ops:
  6.5 98.2 %reduce-scatter.2.cloned.1.call-start = ((), (), s32[]{:S(2)}) async-start(), calls=%async_computation.1 | async-start | bytes 294912 | tf_op jit(solution)/shard_map/reduce_scatter | solution.py:81
  43.0 40.5 %collective-permute-start = (f32[1,4,1,2048]{3,2,1,0:T(1,128)S(1)}, f32[1,4,1,2048]{3,2,1,0:T(1,128)S(1)}, u32[]{:S(2)}, u32[]{:S(2)}) collective-permute-start(f32[1,4,1,2048]{3,2,1,0:T(1,128)S(1)} %get-tuple-element.21), channel_id=1, source_target_pairs={{0,1},{1,2},{2,3},{3,4},{4,5},{5,6},{6,7},{8,9},{9,10},{10,11},{11... | collective-permute-start | bytes 98312 | tf_op jit(solution)/shard_map/ppermute | solution.py:15
  44.9 18.7 %copy-start = (f32[1,2,256,2048]{3,2,1,0:T(8,128)S(1)}, f32[1,2,256,2048]{3,2,1,0:T(8,128)}, u32[]{:S(2)}) copy-start(f32[1,2,256,2048]{3,2,1,0:T(8,128)} %param.9) | copy-start | bytes 12582916
  44.9 38.5 %collective-permute-start.1 = (f32[1,4,1,2048]{3,2,1,0:T(1,128)S(1)}, f32[1,4,1,2048]{3,2,1,0:T(1,128)S(1)}, u32[]{:S(2)}, u32[]{:S(2)}) collective-permute-start(f32[1,4,1,2048]{3,2,1,0:T(1,128)S(1)} %get-tuple-element.20), channel_id=1, source_target_pairs={{1,0},{2,1},{3,2},{4,3},{5,4},{6,5},{7,6},{9,8},{10,9},{11,10},{12... | collective-permute-start | bytes 98312 | tf_op jit(solution)/shard_map/ppermute | solution.py:18
  62.1 5.0 %copy-start.2 = (s32[4]{0:T(128)S(1)}, s32[4]{0:T(128)}, u32[]{:S(2)}) copy-start(s32[4]{0:T(128)} %constant.61.clone.1) | copy-start | bytes 52
  62.1 21.4 %copy-start.1 = (f32[4]{0:T(128)S(1)}, f32[4]{0:T(128)}, u32[]{:S(2)}) copy-start(f32[4]{0:T(128)} %param.10) | copy-start | bytes 52
Sparse Core Ops, SparseCore 0:
  43.1 26.0 reduce-scatter.1
where the time goes:
time: 118 us; the launch traced here: 117 us
  blocking collectives  45 us (38%)
  other arithmetic  29.1 us (25%)
  local copies, waits for them, and re-layouts  22.2 us (19%)
  between operations  13.5 us (11%)
  starting transfers between devices  5.83 us (5%)
  matrix products  1.48 us (1%)
    sub x1, other arithmetic, advance(): return center + diffusivity[None, :, None, None] * laplace - transport  21.2 us
    psum x1, blocking collectives, from_root(): return lax.psum(block, axis)  16.3 us
    slice x2, local copies, waits for them, and re-layouts, advance(): left_cells = jnp.roll(center, 1, axis=3)  14.7 us
    all_gather x1, blocking collectives, shards(): zone_faces = lax.all_gather(own_face, 'slab', axis=0, tiled=True)  14.4 us
    psum x1, blocking collectives, shards(): pin_total = lax.psum(pin_part, 'zone')  14.3 us
    another operation x3, other arithmetic  4.18 us
    ppermute x1, starting transfers between devices, extended(): lax.ppermute(lax.slice_in_dim(block, 0, width, axis=dim), axis, backward)  3.91 us
    mul x1, other arithmetic, advance(): jnp.maximum(along_rows, 0.0) * (center - upper_row)  2.91 us
  transfers between devices with their start and end apart: 3, of which 0 were waited for; matrix products, arithmetic and copies ran while one was open for 35% of the time, Pallas kernels for 0%

commit v1 on v0

--- a/solution.py
+++ b/solution.py
@@ -5,6 +5,12 @@
 
 SEG = 32
 COUPLE = 0.5
+
+
+def draw_scenes(axis_name, xx):
+    moved = lax.all_gather(xx, axis_name=axis_name)
+    w_next = jnp.sum(moved, 0)
+    return w_next
 
 
 def extended(block, sides, width):
@@ -82,7 +88,7 @@
         jnp.dot(picker.T, item_flux, precision=highest), "slab", scatter_dimension=0, tiled=True
     )
     pin_part = jnp.sum(item_flux.reshape(seg_count, fanout, payload), axis=1)
-    pin_total = lax.psum(pin_part, "zone")
+    pin_total = draw_scenes("zone", xx=pin_part)
     is_pin = zone_index == zone_count - 1
     coupling = COUPLE * inflow - jnp.where(is_pin, COUPLE * pin_total, 0.0)
     coupling = (

time: 118 us -> 111 us (0.941)
  blocking collectives: 45 us -> 38.4 us
    psum x1 -> x0, blocking collectives: 14.3 us -> none  [shards(): pin_total = lax.psum(pin_part, 'zone')]
    all_gather x0 -> x1, blocking collectives: none -> 7.64 us  [draw_scenes(): moved = lax.all_gather(xx, axis_name=axis_name)]
  transfers between devices with their start and end apart: 3 -> 3, of which waited for: 0 -> 0; matrix products, arithmetic and copies ran while one was open for 35% -> 38% of each run, Pallas kernels for 0% -> 0%
where the time goes in v1:
time: 111 us
  blocking collectives  38.4 us (35%)
  other arithmetic  29.2 us (26%)
  local copies, waits for them, and re-layouts  22.2 us (20%)
  between operations  13.5 us (12%)
  starting transfers between devices  5.83 us (5%)
  matrix products  1.48 us (1%)
    sub x1, other arithmetic, advance(): return center + diffusivity[None, :, None, None] * laplace - transport  21.2 us
    psum x1, blocking collectives, from_root(): return lax.psum(block, axis)  16.3 us
    slice x2, local copies, waits for them, and re-layouts, advance(): left_cells = jnp.roll(center, 1, axis=3)  14.7 us
    all_gather x1, blocking collectives, shards(): zone_faces = lax.all_gather(own_face, 'slab', axis=0, tiled=True)  14.4 us
    all_gather x1, blocking collectives, draw_scenes(): moved = lax.all_gather(xx, axis_name=axis_name)  7.64 us
    another operation x3, other arithmetic  4.18 us
    ppermute x1, starting transfers between devices, extended(): lax.ppermute(lax.slice_in_dim(block, 0, width, axis=dim), axis, backward)  3.91 us
    mul x1, other arithmetic, advance(): jnp.maximum(along_rows, 0.0) * (center - upper_row)  2.91 us
  transfers between devices with their start and end apart: 3, of which 0 were waited for; matrix products, arithmetic and copies ran while one was open for 38% of the time, Pallas kernels for 0%

profile of v1, /device:TPU:8, one launch (start us, length us, event | category | flops | bytes accessed | tf_op | source)
XLA Modules:
  0.0 110.6 jit_solution(14113195860189836885)
XLA Ops:
  6.5 1.2 %slice_reduce_fusion = (f32[4,2048]{1,0:T(4,128)S(1)}, f32[1,4,1,2048]{3,2,1,0:T(1,128)S(1)}, f32[1,4,1,2048]{3,2,1,0:T(1,128)S(1)}) fusion(f32[1,4,256,2048]{3,2,1,0:T(8,128)} %param.8), kind=kLoop, calls=%fused_computation.45 | loop fusion | bytes 163840 | tf_op jit(solution)/shard_map/slice | solution.py:22
  7.9 14.4 %all_gather.9 = f32[512,128]{1,0:T(8,128)S(1)} all-gather(f32[64,128]{1,0:T(8,128)S(1)} %copy.84), channel_id=1, replica_groups=mesh['zone'=4,'slab'=8] {'slab'}, dimensions={0}, use_global_device_ids=true | all-gather | bytes 294912 | tf_op jit(solution)/shard_map/all_gather | solution.py:80
  22.4 16.3 %psum.7 = f32[64,128]{1,0:T(8,128)S(1)} all-reduce(f32[64,128]{1,0:T(8,128)S(1)} %broadcast_select_fusion.1), channel_id=1, replica_groups=mesh['zone'=4,'slab'=8] {'zone'}, use_global_device_ids=true, to_apply=%region_1.2 | all-reduce | flops 8192 | bytes 65536 | tf_op jit(solution)/shard_map/psum | solution.py:31
  38.7 0.8 copy.80
  39.5 0.1 reshape.148
  39.6 0.8 copy.82
  40.4 0.1 reshape.150
  40.5 0.8 copy.81
  41.3 0.1 reshape.149
  41.5 0.3 fusion.14
  41.8 1.2 %fusion.16 = f32[512,128]{1,0:T(8,128)} fusion(f32[128,128]{1,0:T(8,128)S(1)} %fusion.14, s32[128]{0:T(128)S(1)} %fusion.24, pred[128]{0:T(512)(128)(4,1)S(1)} %get-tuple-element.18), kind=kOutput, calls=%fused_computation.26 | convolution fusion | flops 100794368 | bytes 328320 | tf_op jit(solution)/shard_map/dot_general | solution.py:88
  43.0 1.9 %collective-permute-start = (f32[1,4,1,2048]{3,2,1,0:T(1,128)S(1)}, f32[1,4,1,2048]{3,2,1,0:T(1,128)S(1)}, u32[]{:S(2)}, u32[]{:S(2)}) collective-permute-start(f32[1,4,1,2048]{3,2,1,0:T(1,128)S(1)} %get-tuple-element.21), channel_id=1, source_target_pairs={{0,1},{1,2},{2,3},{3,4},{4,5},{5,6},{6,7},{8,9},{9,10},{10,11},{11... | collective-permute-start | bytes 98312 | tf_op jit(solution)/shard_map/ppermute | solution.py:21
  44.9 3.9 %collective-permute-start.1 = (f32[1,4,1,2048]{3,2,1,0:T(1,128)S(1)}, f32[1,4,1,2048]{3,2,1,0:T(1,128)S(1)}, u32[]{:S(2)}, u32[]{:S(2)}) collective-permute-start(f32[1,4,1,2048]{3,2,1,0:T(1,128)S(1)} %get-tuple-element.20), channel_id=1, source_target_pairs={{1,0},{2,1},{3,2},{4,3},{5,4},{6,5},{7,6},{9,8},{10,9},{11,10},{12... | collective-permute-start | bytes 98312 | tf_op jit(solution)/shard_map/ppermute | solution.py:24
  48.9 13.3 %fusion.28 = (f32[1,4,256,2047]{3,2,1,0:T(8,128)}, f32[1,4,256,2047]{3,2,1,0:T(8,128)}) fusion(f32[1,4,256,2048]{3,2,1,0:T(8,128)} %param.8), kind=kLoop, calls=%fused_computation.47 | loop fusion | bytes 33538048 | tf_op jit(solution)/shard_map/jit(_roll_static)/slice | solution.py:35
  62.1 1.4 %fusion.27 = (f32[1,4,256,1]{3,2,1,0:T(8,128)S(1)}, f32[1,4,256,1]{3,2,1,0:T(8,128)S(1)}) fusion(f32[1,4,256,2048]{3,2,1,0:T(8,128)} %param.8), kind=kLoop, calls=%fused_computation.46 | loop fusion | bytes 16384 | tf_op jit(solution)/shard_map/jit(_roll_static)/slice | solution.py:35
  63.6 2.9 %maximum_bitcast_fusion.1 = (f32[256,2048]{1,0:T(8,128)S(1)}, f32[256,2048]{1,0:T(8,128)}, f32[256,2048]{1,0:T(8,128)}, f32[256,2048]{1,0:T(8,128)}) fusion(f32[1,2,256,2048]{3,2,1,0:T(8,128)S(1)} %copy-done), kind=kLoop, calls=%fused_computation.21 | loop fusion | flops 2097152 | bytes 12582912 | tf_op jit(solution)/shard_map/mul | solution.py:39
  66.5 0.6 fusion.29
  67.1 2.0 %and_reduce_fusion = pred[]{:T(512)} fusion(s32[4]{0:T(128)S(1)} %copy-done.2, s32[1]{0:T(128)} %constant.60.clone.1, s32[1]{0:T(128)} %get-tuple-element.31, s32[1]{0:T(128)} %get-tuple-element.30), kind=kLoop, calls=%fused_computation.36 | loop fusion | flops 27 | bytes 29 | tf_op jit(solution)/shard_map/reduce.1
  69.2 7.6 %all-gather = f32[256,128]{1,0:T(8,128)S(1)} all-gather(f32[64,128]{1,0:T(8,128)S(1)} %reduce_sum.18), channel_id=2, replica_groups=mesh['zone'=4,'slab'=8] {'zone'}, dimensions={0}, use_global_device_ids=true | all-gather | bytes 163840 | tf_op jit(solution)/shard_map/all_gather | solution.py:11
  76.9 21.2 %fusion.6 = f32[1,4,256,2048]{3,2,1,0:T(8,128)} fusion(f32[1,4,256,2048]{3,2,1,0:T(8,128)} %param.8, f32[1,4,1,2048]{3,2,1,0:T(1,128)S(1)} %collective-permute-done.1, f32[1,4,1,2048]{3,2,1,0:T(1,128)S(1)} %collective-permute-done, f32[1,4,256,1]{3,2,1,0:T(8,128)S(1)} %get-tuple-element.23, f32[1,4,256,2047]{3,2,1,0:T(8,128)} %get-tuple-element.25, ...), kind=kLoop, calls=%fused_computation.7 | loop fusion | flops 48234496 | bytes 42008592 | tf_op jit(solution)/shard_map/sub | solution.py:48
  98.1 0.8 select_subtract_fusion
  99.0 0.1 reshape.157
  99.2 2.2 %broadcast_select_fusion = f32[1,4,1,2048]{3,2,1,0:T(1,128)S(1)} fusion(pred[]{:T(512)} %and_reduce_fusion, f32[1,4,1,2048]{3,2,1,0:T(1,128)S(1)} %reshape.157, f32[1,4,256,2048]{3,2,1,0:T(8,128)} %fusion.6, s32[]{:T(128)} %bitcast.4), kind=kLoop, calls=%fused_computation.31 | loop fusion | flops 16384 | bytes 98309 | tf_op jit(solution)/shard_map/select.1
  101.3 2.4 %scatter-add.4 = f32[1,4,256,2048]{3,2,1,0:T(8,128)} dynamic-update-slice(f32[1,4,256,2048]{3,2,1,0:T(8,128)} %fusion.6, f32[1,4,1,2048]{3,2,1,0:T(1,128)S(1)} %broadcast_select_fusion, s32[]{:T(128)} %constant.58.clone.1, s32[]{:T(128)} %constant.58.clone.1, s32[]{:T(128)} %bitcast.4, s32[]{:T(128)} %constant.58.clone.1) | dynamic-update-slice | bytes 65540 | tf_op jit(solution)/shard_map/scatter-add | solution.py:99
  (23 shorter events, 0.6 us)
Async XLA Ops:
  6.5 91.5 %reduce-scatter.2.cloned.1.call-start = ((), (), s32[]{:S(2)}) async-start(), calls=%async_computation.1 | async-start | bytes 294912 | tf_op jit(solution)/shard_map/reduce_scatter | solution.py:87
  43.0 33.8 %collective-permute-start = (f32[1,4,1,2048]{3,2,1,0:T(1,128)S(1)}, f32[1,4,1,2048]{3,2,1,0:T(1,128)S(1)}, u32[]{:S(2)}, u32[]{:S(2)}) collective-permute-start(f32[1,4,1,2048]{3,2,1,0:T(1,128)S(1)} %get-tuple-element.21), channel_id=1, source_target_pairs={{0,1},{1,2},{2,3},{3,4},{4,5},{5,6},{6,7},{8,9},{9,10},{10,11},{11... | collective-permute-start | bytes 98312 | tf_op jit(solution)/shard_map/ppermute | solution.py:21
  44.9 18.7 %copy-start = (f32[1,2,256,2048]{3,2,1,0:T(8,128)S(1)}, f32[1,2,256,2048]{3,2,1,0:T(8,128)}, u32[]{:S(2)}) copy-start(f32[1,2,256,2048]{3,2,1,0:T(8,128)} %param.9) | copy-start | bytes 12582916
  44.9 31.9 %collective-permute-start.1 = (f32[1,4,1,2048]{3,2,1,0:T(1,128)S(1)}, f32[1,4,1,2048]{3,2,1,0:T(1,128)S(1)}, u32[]{:S(2)}, u32[]{:S(2)}) collective-permute-start(f32[1,4,1,2048]{3,2,1,0:T(1,128)S(1)} %get-tuple-element.20), channel_id=1, source_target_pairs={{1,0},{2,1},{3,2},{4,3},{5,4},{6,5},{7,6},{9,8},{10,9},{11,10},{12... | collective-permute-start | bytes 98312 | tf_op jit(solution)/shard_map/ppermute | solution.py:24
  62.1 5.0 %copy-start.2 = (s32[4]{0:T(128)S(1)}, s32[4]{0:T(128)}, u32[]{:S(2)}) copy-start(s32[4]{0:T(128)} %constant.61.clone.1) | copy-start | bytes 52
  62.1 14.7 %copy-start.1 = (f32[4]{0:T(128)S(1)}, f32[4]{0:T(128)}, u32[]{:S(2)}) copy-start(f32[4]{0:T(128)} %param.10) | copy-start | bytes 52
Sparse Core Ops, SparseCore 0:
  43.1 26.0 reduce-scatter.1
